TPU v7x, 32 devices: a whole 2x2x4 slice. The times are simulated.
32 devices in a mesh: group: 2 (over y), frame: 4 (over z), space: 2 (over x), head: 2 (over core).
Axes of the slice: x: 2, y: 2, z: 4, core: 2. Of those that a mesh axis runs over, the one named last changes fastest.
Arguments:
- queries: bfloat16 [8, 8, 48, 3072], P(('group', 'frame'), 'space', None, 'head'), parts along dimension 0, may hold values from -8 to 8
- keys: bfloat16 [8, 8, 48, 3072], P(('group', 'frame'), 'space', None, 'head'), parts along dimension 0, may hold values from -8 to 8
- values: bfloat16 [8, 8, 48, 3072], P(('group', 'frame'), 'space', None, 'head'), parts along dimension 0, may hold values from -6 to 6
- flags: int32 [4, 4], replicated, may hold values from 0 to 1, as said below
- widths: int32 [4], replicated, may hold values from 0 to 8, as said below
Outputs:
- attended: bfloat16 [8, 8, 48, 3072], P(('group', 'frame'), 'space', None, 'head'), parts along dimension 0
There are 2 independent parts, one for each index of `group`. A program takes and returns all parts, laid end to end along the dimension named above; an argument that names none is the same for every part. Nothing has to cross between parts.
Inputs may be any that keep to these rules, and one draw needn't show every extreme that they name: flags[f, g] = 1 wherever |f - g| <= 1, and flags[0, 3] = flags[3, 0] = 0. widths[0] = 8, and widths never rise with the frame distance.
All inputs are finite; a program needn't handle non-finite values.
Results may differ from a plain program's by a relative error of at most 0.006.
Values may be sent and summed in bfloat16 or wider, within the bound.
A program may use at most 128 MiB of HBM per device.

v0:
```python
import jax
import jax.numpy as jnp
from jax import lax
from jax.sharding import PartitionSpec as P

HEAD_DIM = 128


NEG_FILL = -1e30


def empty_state(leading, head_count, query_count):
    return (
        jnp.full(leading + (head_count, query_count), NEG_FILL, jnp.float32),
        jnp.zeros(leading + (head_count, query_count), jnp.float32),
        jnp.zeros(leading + (head_count, query_count, HEAD_DIM), jnp.float32),
    )


def block_update(state_old, query_heads, query_rows, reach_rows, key_block, key_rows):
    running_max, running_total, running_acc = state_old
    query_count, head_count, head_size = query_heads.shape
    key_count = key_rows.shape[0]
    score_scale = 1.0 / HEAD_DIM**0.5
    allowed = jnp.abs(query_rows[:, None] - key_rows[None, :]) <= reach_rows
    key_heads = key_block[0].reshape(key_count, head_count, head_size)
    value_heads = key_block[1].reshape(key_count, head_count, head_size)
    scores = (
        jnp.einsum("qhd,khd->hqk", query_heads, key_heads, preferred_element_type=jnp.float32)
        * score_scale
    )
    scores = jnp.where(allowed[None], scores, NEG_FILL)
    new_max = jnp.maximum(running_max, jnp.max(scores, axis=2))
    weights = jnp.where(allowed[None], jnp.exp(scores - new_max[:, :, None]), 0.0)
    rescale = jnp.exp(running_max - new_max)
    new_total = running_total * rescale + jnp.sum(weights, axis=2)
    new_acc = running_acc * rescale[:, :, None] + jnp.einsum(
        "hqk,khd->hqd",
        weights.astype(jnp.bfloat16),
        value_heads,
        preferred_element_type=jnp.float32,
    )
    return (new_max, new_total, new_acc)


def shards(queries, keys, values, flags, widths):
    frame_now = lax.axis_index("frame")
    head_query, head_key, head_value = (
        lax.all_to_all(queries, "space", split_axis=3, concat_axis=1, tiled=True),
        lax.all_to_all(keys, "space", split_axis=3, concat_axis=1, tiled=True),
        lax.all_to_all(values, "space", split_axis=3, concat_axis=1, tiled=True),
    )
    row_total = head_query.shape[1]
    columns = head_query.shape[2]
    features = head_query.shape[3]
    head_count = features // HEAD_DIM
    frame_tokens = row_total * columns
    key_rows = jnp.arange(frame_tokens, dtype=jnp.int32) // columns
    stacked = jnp.stack(
        [head_key.reshape(frame_tokens, features), head_value.reshape(frame_tokens, features)],
        axis=0,
    )[None]
    query_heads = head_query.reshape(frame_tokens, head_count, HEAD_DIM)
    flag_row = lax.dynamic_index_in_dim(flags, frame_now, 0, False)
    initial = empty_state((), head_count, frame_tokens)
    key_piece = lax.all_gather(stacked, "frame", axis=0, tiled=True)

    def advance(state_old, step_items):
        key_block, offset_now = step_items
        reach_rows = lax.dynamic_index_in_dim(widths, jnp.abs(frame_now - offset_now), 0, False)
        flag_now = lax.dynamic_index_in_dim(flag_row, offset_now, 0, False)
        state_new = lax.cond(
            flag_now > 0,
            lambda kept_state: block_update(
                kept_state, query_heads, key_rows, reach_rows, key_block, key_rows
            ),
            lambda kept_state: kept_state,
            state_old,
        )
        return (state_new, None)

    state_new, unused = lax.scan(
        advance, initial, (key_piece, jnp.arange(key_piece.shape[0], dtype=jnp.int32))
    )
    final_max, final_total, final_acc = state_new
    blended = final_acc / final_total[:, :, None]
    joined = jnp.transpose(blended, (1, 0, 2)).reshape(head_query.shape).astype(jnp.bfloat16)
    return lax.all_to_all(joined, "space", split_axis=1, concat_axis=3, tiled=True)


def solution(mesh):
    placed = (
        P(("group", "frame"), "space", None, "head"),
        P(("group", "frame"), "space", None, "head"),
        P(("group", "frame"), "space", None, "head"),
        P(),
        P(),
    )
    return jax.shard_map(
        shards,
        mesh=mesh,
        in_specs=placed,
        out_specs=P(("group", "frame"), "space", None, "head"),
        check_vma=False,
    )
```

profile of v0, /device:TPU:0, one launch (start us, length us, event | category | flops | bytes accessed | tf_op | source)
XLA Modules:
  0.0 196.1 jit_solution(7581698430664993695)
XLA Ops:
  6.5 2.6 %copy.41 = bf16[1,4,48,1536]{2,1,0,3:T(4,128)(2,1)S(1)} copy(bf16[1,4,48,1536]{3,2,1,0:T(8,128)(2,1)} %param.11) | data formatting | bytes 1179648 | tf_op args[2]
  9.1 3.4 %reshape.68 = bf16[2,2,73728]{2,1,0:T(2,128)(2,1)} reshape(bf16[1536,1,4,48]{3,2,1,0:T(4,128)(2,1)S(1)} %bitcast.61) | data formatting | bytes 1179648
  12.5 4.2 %all-to-all-start.1 = ((bf16[2,2,73728]{2,1,0:T(2,128)(2,1)}), bf16[2,2,73728]{2,1,0:T(2,128)(2,1)S(1)}, u32[]{:S(2)}, u32[]{:S(2)}) async-start(bf16[2,2,73728]{2,1,0:T(2,128)(2,1)} %reshape.68), calls=%async_computation.1 | async-start | bytes 1179648 | tf_op jit(solution)/shard_map/all_to_all | solution.py:51
  17.8 3.4 %reshape.70 = bf16[2,2,73728]{2,1,0:T(2,128)(2,1)} reshape(bf16[1536,1,4,48]{3,2,1,0:T(4,128)(2,1)S(1)} %bitcast.62) | data formatting | bytes 1179648
  21.2 5.0 %all-to-all-done.1 = bf16[2,2,73728]{2,1,0:T(2,128)(2,1)S(1)} async-done(((bf16[2,2,73728]{2,1,0:T(2,128)(2,1)}), bf16[2,2,73728]{2,1,0:T(2,128)(2,1)S(1)}, u32[]{:S(2)}, u32[]{:S(2)}) %all-to-all-start.1) | async-done | bytes 589856 | tf_op jit(solution)/shard_map/all_to_all | solution.py:51
  26.2 3.5 %all-to-all-start = ((bf16[2,2,73728]{2,1,0:T(2,128)(2,1)}), bf16[2,2,73728]{2,1,0:T(2,128)(2,1)S(1)}, u32[]{:S(2)}, u32[]{:S(2)}) async-start(bf16[2,2,73728]{2,1,0:T(2,128)(2,1)} %reshape.70), calls=%async_computation | async-start | bytes 1179648 | tf_op jit(solution)/shard_map/all_to_all | solution.py:50
  29.8 1.6 reshape.69
  32.8 5.3 %all-to-all-done = bf16[2,2,73728]{2,1,0:T(2,128)(2,1)S(1)} async-done(((bf16[2,2,73728]{2,1,0:T(2,128)(2,1)}), bf16[2,2,73728]{2,1,0:T(2,128)(2,1)S(1)}, u32[]{:S(2)}, u32[]{:S(2)}) %all-to-all-start) | async-done | bytes 589856 | tf_op jit(solution)/shard_map/all_to_all | solution.py:50
  38.1 1.6 reshape.71
  43.3 3.4 %reshape.72 = bf16[2,2,73728]{2,1,0:T(2,128)(2,1)} reshape(bf16[1536,1,4,48]{3,2,1,0:T(4,128)(2,1)S(1)} %bitcast.63) | data formatting | bytes 1179648
  46.7 3.7 %all-to-all-start.2 = ((bf16[2,2,73728]{2,1,0:T(2,128)(2,1)}), bf16[2,2,73728]{2,1,0:T(2,128)(2,1)S(1)}, u32[]{:S(2)}, u32[]{:S(2)}) async-start(bf16[2,2,73728]{2,1,0:T(2,128)(2,1)} %reshape.72), calls=%async_computation.2 | async-start | bytes 1179648 | tf_op jit(solution)/shard_map/all_to_all | solution.py:49
  50.4 7.3 %all-to-all-done.2 = bf16[2,2,73728]{2,1,0:T(2,128)(2,1)S(1)} async-done(((bf16[2,2,73728]{2,1,0:T(2,128)(2,1)}), bf16[2,2,73728]{2,1,0:T(2,128)(2,1)S(1)}, u32[]{:S(2)}, u32[]{:S(2)}) %all-to-all-start.2) | async-done | bytes 589856 | tf_op jit(solution)/shard_map/all_to_all | solution.py:49
  57.7 1.6 reshape.73
  60.8 71.3 %all-gather.3.cloned.1.call-done = bf16[8,384,768]{2,1,0:T(8,128)(2,1)} async-done(((bf16[2,384,768]{2,1,0:T(8,128)(2,1)}), bf16[8,384,768]{2,1,0:T(8,128)(2,1)}) %all-gather.3.cloned.1.call-update) | async-done | bytes 4718608 | tf_op jit(solution)/shard_map/all_gather | solution.py:66
  132.1 6.6 %copy.46 = bf16[4,2,384,768]{2,3,1,0:T(8,128)(2,1)} copy(bf16[4,2,384,768]{3,2,1,0:T(8,128)(2,1)} %bitcast.64) | data formatting | bytes 9437184
  138.8 36.8 %while.15 = (s32[]{:T(128)}, f32[6,384]{1,0:T(8,128)S(1)}, f32[6,384]{1,0:T(8,128)S(1)}, f32[6,384,128]{2,1,0:T(8,128)S(1)}, s32[4]{0:T(128)S(1)}, /*index=5*/s3...) while((s32[]{:T(128)}, f32[6,384]{1,0:T(8,128)S(1)}, ...), condition=%wide.region_5.6_spmd.clone, body=%wide.region_0.5_spmd.clone.sunk | while | flops 465526272 | bytes 17858036 | solution.py:82
  142.7 7.1 %conditional.3 = ((f32[6,384]{1,0:T(8,128)S(1)}, f32[6,384]{1,0:T(8,128)S(1)}, f32[6,384,128]{2,1,0:T(8,128)S(1)})) conditional(s32[]{:T(128)} %bitcast.55, (f32[6,384]{1,0:T(8,128)S(1)}, f32[6,384]{1,0:T(8,128)S(1)}, f32[6,384,128]{2,1,0:T(8,128)S(1)}) %tuple.48, (s32[384]{0:T(512)S(1)}, s32[]{:T(128)}, s32[]{:T(128)}, s32[4]{0:T(128)S(1)}, ...), branch_computations={%region_1.1_spmd, %region_2.4_spmd.clone} | conditional | flops 465525888 | bytes 17853058 | solution.py:72
  144.9 1.4 constant_dynamic-slice_fusion.1
  148.1 1.7 fusion.12
  153.7 7.1 %conditional.3 = ((f32[6,384]{1,0:T(8,128)S(1)}, f32[6,384]{1,0:T(8,128)S(1)}, f32[6,384,128]{2,1,0:T(8,128)S(1)})) conditional(s32[]{:T(128)} %bitcast.55, (f32[6,384]{1,0:T(8,128)S(1)}, f32[6,384]{1,0:T(8,128)S(1)}, f32[6,384,128]{2,1,0:T(8,128)S(1)}) %tuple.48, (s32[384]{0:T(512)S(1)}, s32[]{:T(128)}, s32[]{:T(128)}, s32[4]{0:T(128)S(1)}, ...), branch_computations={%region_1.1_spmd, %region_2.4_spmd.clone} | conditional | flops 465525888 | bytes 17853058 | solution.py:72
  159.1 1.7 fusion.12
  164.6 7.1 %conditional.3 = ((f32[6,384]{1,0:T(8,128)S(1)}, f32[6,384]{1,0:T(8,128)S(1)}, f32[6,384,128]{2,1,0:T(8,128)S(1)})) conditional(s32[]{:T(128)} %bitcast.55, (f32[6,384]{1,0:T(8,128)S(1)}, f32[6,384]{1,0:T(8,128)S(1)}, f32[6,384,128]{2,1,0:T(8,128)S(1)}) %tuple.48, (s32[384]{0:T(512)S(1)}, s32[]{:T(128)}, s32[]{:T(128)}, s32[4]{0:T(128)S(1)}, ...), branch_computations={%region_1.1_spmd, %region_2.4_spmd.clone} | conditional | flops 465525888 | bytes 17853058 | solution.py:72
  170.0 1.7 fusion.12
  177.1 11.3 %all_to_all.63 = bf16[1,8,48,768]{3,2,0,1:T(8,128)(2,1)S(1)} all-to-all(bf16[1,8,48,768]{3,2,0,1:T(8,128)(2,1)S(1)} %bitcast.70), channel_id=1, replica_groups=mesh['group'=2,'frame'=4,'space'=2,'head'=2] {'space'}, dimensions={1} | all-to-all | bytes 1179648 | tf_op jit(solution)/shard_map/all_to_all | solution.py:88
  (76 shorter events, 27.7 us)
Async XLA Ops:
  6.5 43.9 %copy-start = (s32[4,4]{1,0:T(4,128)S(1)}, s32[4,4]{1,0:T(4,128)}, u32[]{:S(2)}) copy-start(s32[4,4]{1,0:T(4,128)} %param.12) | copy-start | bytes 196
  6.5 10.2 %copy-start.1 = (bf16[1,4,48,1536]{3,2,1,0:T(8,128)(2,1)S(1)}, bf16[1,4,48,1536]{3,2,1,0:T(8,128)(2,1)}, u32[]{:S(2)}) copy-start(bf16[1,4,48,1536]{3,2,1,0:T(8,128)(2,1)} %param.10) | copy-start | bytes 1769476
  12.5 13.7 %all-to-all-start.1 = ((bf16[2,2,73728]{2,1,0:T(2,128)(2,1)}), bf16[2,2,73728]{2,1,0:T(2,128)(2,1)S(1)}, u32[]{:S(2)}, u32[]{:S(2)}) async-start(bf16[2,2,73728]{2,1,0:T(2,128)(2,1)} %reshape.68), calls=%async_computation.1 | async-start | bytes 1179648 | tf_op jit(solution)/shard_map/all_to_all | solution.py:51
  26.2 11.9 %all-to-all-start = ((bf16[2,2,73728]{2,1,0:T(2,128)(2,1)}), bf16[2,2,73728]{2,1,0:T(2,128)(2,1)S(1)}, u32[]{:S(2)}, u32[]{:S(2)}) async-start(bf16[2,2,73728]{2,1,0:T(2,128)(2,1)} %reshape.70), calls=%async_computation | async-start | bytes 1179648 | tf_op jit(solution)/shard_map/all_to_all | solution.py:50
  29.7 102.4 %all-gather.3.cloned.1.call-start = ((), (), s32[]{:S(2)}) async-start(), calls=%async_computation.4 | async-start | bytes 5898240 | tf_op jit(solution)/shard_map/all_gather | solution.py:66
  39.6 2.6 %copy-start.2 = (bf16[1,4,48,1536]{3,2,1,0:T(8,128)(2,1)S(1)}, bf16[1,4,48,1536]{3,2,1,0:T(8,128)(2,1)}, u32[]{:S(2)}) copy-start(bf16[1,4,48,1536]{3,2,1,0:T(8,128)(2,1)} %param.9) | copy-start | bytes 1769476
  46.7 11.0 %all-to-all-start.2 = ((bf16[2,2,73728]{2,1,0:T(2,128)(2,1)}), bf16[2,2,73728]{2,1,0:T(2,128)(2,1)S(1)}, u32[]{:S(2)}, u32[]{:S(2)}) async-start(bf16[2,2,73728]{2,1,0:T(2,128)(2,1)} %reshape.72), calls=%async_computation.2 | async-start | bytes 1179648 | tf_op jit(solution)/shard_map/all_to_all | solution.py:49
  132.1 6.7 %copy-start.3 = (s32[4]{0:T(128)S(1)}, s32[4]{0:T(128)}, u32[]{:S(2)}) copy-start(s32[4]{0:T(128)} %param.13) | copy-start | bytes 52
Sparse Core Ops, SparseCore 0:
  42.4 89.6 all-gather.2
where the time goes:
time: 195 us; the launch traced here: 196 us
  waiting for transfers between devices  88.9 us (46%)
  local copies, waits for them, and re-layouts  43.4 us (22%)
  between operations  13.6 us (7%)
  loops' own time  12.7 us (7%)
  starting transfers between devices  11.5 us (6%)
  blocking collectives  11.3 us (6%)
  matrix products  7.69 us (4%)
  other arithmetic  7.04 us (4%)
    all_gather x1, waiting for transfers between devices, shards(): key_piece = lax.all_gather(stacked, 'frame', axis=0, tiled=True)  71.3 us
    unnamed x19, local copies, waits for them, and re-layouts  26.3 us
    all_to_all x1, blocking collectives, shards(): lax.all_to_all(joined, 'space', split_axis=1, concat_axis=3, tiled=True)  11.3 us
    another operation x1, loops' own time, shards(): lax.scan(advance, initial, (key_piece, jnp.arange(key_piece.shape[0], dty...  10.5 us
    all_to_all x1, waiting for transfers between devices, shards(): lax.all_to_all(queries, 'space', split_axis=3, concat_axis=1, tiled=True)  7.27 us
    all_to_all x1, waiting for transfers between devices, shards(): lax.all_to_all(keys, 'space', split_axis=3, concat_axis=1, tiled=True)  5.31 us
    dot_general x3, matrix products, block_update(): jnp.einsum('hqk,khd->hqd', weights.astype(jnp.bfloat16), value_heads, pre...  5.05 us
    all_to_all x1, waiting for transfers between devices, shards(): lax.all_to_all(values, 'space', split_axis=3, concat_axis=1, tiled=True)  5 us
  transfers between devices with their start and end apart: 4, of which 4 were waited for; matrix products, arithmetic and copies ran while one was open for 8% of the time, Pallas kernels for 0%

commit v1 on v0

v1 whole, which is shorter than its diff:
```python
import functools
import math

import jax
import jax.numpy as jnp
from jax import lax
from jax.experimental import pallas as pl
from jax.experimental.pallas import tpu as pltpu
from jax.sharding import PartitionSpec as P

HEAD_DIM = 128
NEG_FILL = -1e30
SCALE = math.log2(math.e) / HEAD_DIM**0.5
MESH = pl.DeviceIdType.MESH


def kernel(
    frames,
    parts,
    heads,
    q_ref,
    k_ref,
    v_ref,
    flags_ref,
    widths_ref,
    row_ref,
    col_ref,
    out_ref,
    kv,
    qb,
    ob,
    dist,
    top,
    total,
    acc,
    local_sem,
    xkv_send,
    xkv_recv,
    xq_send,
    xq_recv,
    z_send,
    z_recv,
    o_local,
    o_send,
    o_recv,
):
    frame = lax.axis_index("frame")
    part = lax.axis_index("space")
    rows = q_ref.shape[0]
    tokens = parts * rows
    tile = 128 if tokens % 128 == 0 else rows
    far = frames - 2
    LEFT, RIGHT = 0, 1

    def lanes(ref, head):
        return ref.at[:, pl.ds(pl.multiple_of(head * HEAD_DIM, HEAD_DIM), HEAD_DIM)]

    def peer(j):
        return lax.rem(part + j, parts)

    barrier = pltpu.get_barrier_semaphore()
    for j in range(1, parts):
        pl.semaphore_signal(barrier, inc=1, device_id={"space": peer(j)}, device_id_type=MESH)

    @pl.when(frame > 0)
    def _():
        pl.semaphore_signal(barrier, inc=1, device_id={"frame": frame - 1}, device_id_type=MESH)

    @pl.when(frame < frames - 1)
    def _():
        pl.semaphore_signal(barrier, inc=1, device_id={"frame": frame + 1}, device_id_type=MESH)

    def local_copies(h):
        mine = part * heads + h
        return (
            pltpu.make_async_copy(lanes(k_ref, mine), kv.at[frame, h, part, 0], local_sem.at[0, h]),
            pltpu.make_async_copy(lanes(v_ref, mine), kv.at[frame, h, part, 1], local_sem.at[1, h]),
            pltpu.make_async_copy(lanes(q_ref, mine), qb.at[h, part], local_sem.at[2, h]),
        )

    def kv_exchange(h, j, i, src_ref):
        return pltpu.make_async_remote_copy(
            src_ref=lanes(src_ref, peer(j) * heads + h),
            dst_ref=kv.at[frame, h, part, i],
            send_sem=xkv_send.at[i, j - 1, h],
            recv_sem=xkv_recv.at[i, j - 1, h],
            device_id={"space": peer(j)},
            device_id_type=MESH,
        )

    def q_exchange(h, j):
        return pltpu.make_async_remote_copy(
            src_ref=lanes(q_ref, peer(j) * heads + h),
            dst_ref=qb.at[h, part],
            send_sem=xq_send.at[j - 1, h],
            recv_sem=xq_recv.at[j - 1, h],
            device_id={"space": peer(j)},
            device_id_type=MESH,
        )

    def o_exchange(h, j):
        return pltpu.make_async_remote_copy(
            src_ref=ob.at[h, pl.ds(pl.multiple_of(peer(j) * rows, rows), rows)],
            dst_ref=lanes(out_ref, part * heads + h),
            send_sem=o_send.at[j - 1, h],
            recv_sem=o_recv.at[j - 1, h],
            device_id={"space": peer(j)},
            device_id_type=MESH,
        )

    def o_keep(h):
        return pltpu.make_async_copy(
            ob.at[h, pl.ds(pl.multiple_of(part * rows, rows), rows)],
            lanes(out_ref, part * heads + h),
            o_local.at[h],
        )

    def hop(side, step, h, p, i, src=None):
        towards = 1 if side == RIGHT else -1
        owner = frame - towards * (step - 1)
        return pltpu.make_async_remote_copy(
            src_ref=kv.at[owner, h, p, i] if src is None else src,
            dst_ref=kv.at[owner, h, p, i],
            send_sem=z_send.at[side, step - 1, h, p, i],
            recv_sem=z_recv.at[side, step - 1, h, p, i],
            device_id={"frame": frame + towards},
            device_id_type=MESH,
        )

    def can_send(side, step):
        if side == RIGHT:
            return (frame < frames - 1) & (frame - (step - 1) >= 0)
        return (frame > 0) & (frame + (step - 1) <= frames - 1)

    def gets(side, step):
        if side == RIGHT:
            return frame - step >= 0
        return frame + step <= frames - 1

    def landed(side, step, h, p, i):
        towards = 1 if side == RIGHT else -1
        owner = frame - towards * step
        return pltpu.make_async_remote_copy(
            src_ref=kv.at[owner, h, p, i],
            dst_ref=kv.at[owner, h, p, i],
            send_sem=z_send.at[side, step - 1, h, p, i],
            recv_sem=z_recv.at[side, step - 1, h, p, i],
            device_id={"frame": frame - towards},
            device_id_type=MESH,
        )

    def each_head(body):
        @pl.loop(0, heads)
        def _(h):
            body(h)

    pl.semaphore_wait(
        barrier,
        parts - 1 + jnp.where(frame > 0, 1, 0) + jnp.where(frame < frames - 1, 1, 0),
    )

    def open_head(h):
        mine = part * heads + h
        for j in range(1, parts):
            kv_exchange(h, j, 0, k_ref).start()
            kv_exchange(h, j, 1, v_ref).start()
        for side in (LEFT, RIGHT):

            @pl.when(can_send(side, 1))
            def _():
                hop(side, 1, h, part, 0, lanes(k_ref, mine)).start()
                hop(side, 1, h, part, 1, lanes(v_ref, mine)).start()

    each_head(open_head)

    def open_queries(h):
        for copy in local_copies(h):
            copy.start()
        for j in range(1, parts):
            q_exchange(h, j).start()

    each_head(open_queries)

    dist[...] = jnp.abs(row_ref[...] - col_ref[...])
    top[...] = jnp.full(top.shape, NEG_FILL, jnp.float32)
    total[...] = jnp.zeros(total.shape, jnp.float32)
    acc[...] = jnp.zeros(acc.shape, jnp.float32)

    def pass_parts(h):
        for j in range(1, parts):
            p = lax.rem(part - j + parts, parts)
            for i in (0, 1):
                kv_exchange(h, j, i, (k_ref, v_ref)[i]).wait_recv()
            for side in (LEFT, RIGHT):

                @pl.when(can_send(side, 1))
                def _():
                    for i in (0, 1):
                        hop(side, 1, h, p, i).start()

    each_head(pass_parts)

    def update(h, g):
        gap = jnp.abs(frame - g)
        reach = jnp.where(flags_ref[frame, g] > 0, widths_ref[gap], -1)
        keys = kv[g, h, :, 0].reshape(tokens, HEAD_DIM)
        vals = kv[g, h, :, 1].reshape(tokens, HEAD_DIM)
        queries = qb[h].reshape(tokens, HEAD_DIM)
        for at in range(0, tokens, tile):
            cut = pl.ds(at, tile)
            scores = lax.dot_general(
                queries[at : at + tile],
                keys,
                (((1,), (1,)), ((), ())),
                preferred_element_type=jnp.float32,
            )
            scores = jnp.where(dist[cut, :] <= reach, scores, NEG_FILL)
            old_top = top[h, cut]
            new_top = jnp.maximum(old_top, jnp.max(scores, axis=1, keepdims=True))
            weights = jnp.exp2((scores - new_top) * SCALE)
            keep = jnp.exp2((old_top - new_top) * SCALE)
            top[h, cut] = new_top
            total[h, cut] = total[h, cut] * keep + jnp.sum(weights, axis=1, keepdims=True)
            acc[h, cut] = acc[h, cut] * keep + jnp.dot(
                weights.astype(jnp.bfloat16), vals, preferred_element_type=jnp.float32
            )

    def arrive(step, h):
        for side in (LEFT, RIGHT):

            @pl.when(gets(side, step))
            def _():
                for p in range(parts):
                    for i in (0, 1):
                        landed(side, step, h, p, i).wait_recv()

            if step < far:

                @pl.when(gets(side, step) & can_send(side, step + 1))
                def _():
                    for p in range(parts):
                        for i in (0, 1):
                            hop(side, step + 1, h, p, i).start()

    def blend(step, h):
        @pl.when(frame - step >= 0)
        def _():
            update(h, frame - step)

        @pl.when(frame + step <= frames - 1)
        def _():
            update(h, frame + step)

    for step in range(1, far + 1):

        def advance(h, step=step):
            arrive(step, h)
            if step == 1:
                for copy in local_copies(h):
                    copy.wait()
                for j in range(1, parts):
                    q_exchange(h, j).wait_recv()
                update(h, frame)
            blend(step, h)
            if step == far:
                ob[h] = (acc[h] / total[h]).astype(jnp.bfloat16)
                for j in range(1, parts):
                    o_exchange(h, j).start()
                o_keep(h).start()

        each_head(advance)

    def close_head(h):
        mine = part * heads + h
        o_keep(h).wait()
        for j in range(1, parts):
            o_exchange(h, j).wait()
            q_exchange(h, j).wait_send()
            kv_exchange(h, j, 0, k_ref).wait_send()
            kv_exchange(h, j, 1, v_ref).wait_send()
        for step in range(1, far + 1):
            for side in (LEFT, RIGHT):

                @pl.when(can_send(side, step))
                def _():
                    for p in range(parts):
                        for i in (0, 1):
                            hop(side, step, h, p, i).wait_send()

    each_head(close_head)


def shards(frames, parts, queries, keys, values, flags, widths):
    shape = queries.shape
    columns, features = shape[2], shape[3]
    rows = shape[1] * columns
    heads = features // HEAD_DIM // parts
    tokens = rows * parts
    far = frames - 2
    token_rows = jnp.arange(tokens, dtype=jnp.int32) // columns
    flat = [a.reshape(rows, features) for a in (queries, keys, values)]
    any_spec = pl.BlockSpec(memory_space=pl.ANY)
    vmem = pl.BlockSpec(memory_space=pltpu.VMEM)
    smem = pl.BlockSpec(memory_space=pltpu.SMEM)
    others = max(parts - 1, 1)
    dma = pltpu.SemaphoreType.DMA
    out = pl.pallas_call(
        functools.partial(kernel, frames, parts, heads),
        out_shape=jax.ShapeDtypeStruct((rows, features), jnp.bfloat16),
        in_specs=[any_spec, any_spec, any_spec, smem, smem, vmem, vmem],
        out_specs=any_spec,
        scratch_shapes=[
            pltpu.VMEM((frames, heads, parts, 2, rows, HEAD_DIM), jnp.bfloat16),
            pltpu.VMEM((heads, parts, rows, HEAD_DIM), jnp.bfloat16),
            pltpu.VMEM((heads, tokens, HEAD_DIM), jnp.bfloat16),
            pltpu.VMEM((tokens, tokens), jnp.int32),
            pltpu.VMEM((heads, tokens, 1), jnp.float32),
            pltpu.VMEM((heads, tokens, 1), jnp.float32),
            pltpu.VMEM((heads, tokens, HEAD_DIM), jnp.float32),
            dma((3, heads)),
            dma((2, others, heads)),
            dma((2, others, heads)),
            dma((others, heads)),
            dma((others, heads)),
            dma((2, far, heads, parts, 2)),
            dma((2, far, heads, parts, 2)),
            dma((heads,)),
            dma((others, heads)),
            dma((others, heads)),
        ],
        compiler_params=pltpu.CompilerParams(collective_id=0, has_side_effects=True),
    )(*flat, flags, widths, token_rows[:, None], token_rows[None, :])
    return out.reshape(shape)


def solution(mesh):
    spec = P(("group", "frame"), "space", None, "head")
    return jax.shard_map(
        functools.partial(shards, mesh.shape["frame"], mesh.shape["space"]),
        mesh=mesh,
        in_specs=(spec, spec, spec, P(), P()),
        out_specs=spec,
        check_vma=False,
    )
```

time: 195 us -> 67.5 us (0.35)
  waiting for transfers between devices: 88.9 us -> 0 us
  Pallas kernels: 0 us -> 64.1 us
  local copies, waits for them, and re-layouts: 43.4 us -> 1.92 us
  between operations: 13.6 us -> 0.01 us
  loops' own time: 12.7 us -> 0 us
  starting transfers between devices: 11.5 us -> 0 us
  blocking collectives: 11.3 us -> 0 us
  matrix products: 7.69 us -> 0 us
  other arithmetic: 7.04 us -> 1.31 us
    all_gather x1 -> x0, waiting for transfers between devices: 71.3 us -> none  [shards(): key_piece = lax.all_gather(stacked, 'frame', axis=0, tiled=True)]
    pallas_call x0 -> x1, Pallas kernels: none -> 64.1 us  [shards(): pl.pallas_call(functools.partial(kernel, frames, parts, heads), out_shape...]
    unnamed x19 -> x1, local copies, waits for them, and re-layouts: 26.3 us -> 1.92 us
    all_to_all x3 -> x0, waiting for transfers between devices: 17.6 us -> none  [the longest x1 7.27 us: shards(): lax.all_to_all(queries, 'space', split_axis=3, concat_axis=1, tiled=True)]
    another operation x5 -> x0, loops' own time: 12.7 us -> none  [the longest x1 10.5 us: shards(): lax.scan(advance, initial, (key_piece, jnp.arange(key_piece.shape[0], dty...]
    all_to_all x3 -> x0, starting transfers between devices: 11.4 us -> none  [the longest x1 4.23 us: shards(): lax.all_to_all(values, 'space', split_axis=3, concat_axis=1, tiled=True)]
    all_to_all x1 -> x0, blocking collectives: 11.3 us -> none  [shards(): lax.all_to_all(joined, 'space', split_axis=1, concat_axis=3, tiled=True)]
    dot_general x6 -> x0, matrix products: 7.69 us -> none  [the longest x3 5.05 us: block_update(): jnp.einsum('hqk,khd->hqd', weights.astype(jnp.bfloat16), value_heads, pre...]
  transfers between devices with their start and end apart: 4 -> 0, of which waited for: 4 -> 0; matrix products, arithmetic and copies ran while one was open for 8% -> 0% of each run, Pallas kernels for 0% -> 0%
where the time goes in v1:
time: 67.5 us; the launch traced here: 67.3 us
  Pallas kernels  64.1 us (95%)
  local copies, waits for them, and re-layouts  1.92 us (3%)
  other arithmetic  1.31 us (2%)
    pallas_call x1, Pallas kernels, shards(): pl.pallas_call(functools.partial(kernel, frames, parts, heads), out_shape...  64.1 us
    unnamed x1, local copies, waits for them, and re-layouts  1.92 us

profile of v1, /device:TPU:0, one launch (start us, length us, event | category | flops | bytes accessed | tf_op | source)
XLA Modules:
  0.0 67.3 jit_solution(18218199287674791202)
XLA Ops:
  0.0 0.6 and_select_fusion.col_ref
  0.6 0.7 %add_select_fusion.row_ref = s32[384,1]{1,0:T(8,128)} fusion(), kind=kLoop, calls=%fused_computation.3 | loop fusion | flops 3072 | bytes 1536 | tf_op jit(solution)/shard_map/jit(floor_divide)/jit(_where)/select_n | solution.py:300
  1.3 64.1 %shard_map.55 = bf16[192,1536]{1,0:T(8,128)(2,1)} custom-call(bf16[192,1536]{1,0:T(8,128)(2,1)} %bitcast.5, bf16[192,1536]{1,0:T(8,128)(2,1)} %bitcast.6, bf16[192,1536]{1,0:T(8,128)(2,1)} %bitcast.7, s32[4,4]{1,0:T(4,128)} %flags_ref.1, s32[4]{0:T(128)} %widths_ref.1, s32[384,1]{1,0:T(8,128)} %add_select_fusion.row_ref, s32[1,384]{1,0:T(1,128)} %and_select_fusion.col_ref), custom_call_target="tpu_custom_call" | custom-call | tf_op jit(solution)/shard_map/pallas_call | solution.py:307
  65.4 1.9 %copy.7 = bf16[1,4,48,1536]{3,2,1,0:T(8,128)(2,1)} copy(bf16[1,4,48,1536]{3,2,1,0:T(8,128)(2,1)} %bitcast.4) | data formatting | bytes 1179648

commit v2 on v1

--- a/solution.py
+++ b/solution.py
@@ -18,18 +18,18 @@
     frames,
     parts,
     heads,
+    columns,
     q_ref,
     k_ref,
     v_ref,
     flags_ref,
     widths_ref,
-    row_ref,
-    col_ref,
     out_ref,
     kv,
     qb,
     ob,
     dist,
+    wb,
     top,
     total,
     acc,
@@ -48,7 +48,7 @@
     part = lax.axis_index("space")
     rows = q_ref.shape[0]
     tokens = parts * rows
-    tile = 128 if tokens % 128 == 0 else rows
+    tile = rows
     far = frames - 2
     LEFT, RIGHT = 0, 1
 
@@ -73,15 +73,15 @@
     def local_copies(h):
         mine = part * heads + h
         return (
-            pltpu.make_async_copy(lanes(k_ref, mine), kv.at[frame, h, part, 0], local_sem.at[0, h]),
-            pltpu.make_async_copy(lanes(v_ref, mine), kv.at[frame, h, part, 1], local_sem.at[1, h]),
+            pltpu.make_async_copy(lanes(k_ref, mine), kv.at[frame, h, 0, part], local_sem.at[0, h]),
+            pltpu.make_async_copy(lanes(v_ref, mine), kv.at[frame, h, 1, part], local_sem.at[1, h]),
             pltpu.make_async_copy(lanes(q_ref, mine), qb.at[h, part], local_sem.at[2, h]),
         )
 
     def kv_exchange(h, j, i, src_ref):
         return pltpu.make_async_remote_copy(
             src_ref=lanes(src_ref, peer(j) * heads + h),
-            dst_ref=kv.at[frame, h, part, i],
+            dst_ref=kv.at[frame, h, i, part],
             send_sem=xkv_send.at[i, j - 1, h],
             recv_sem=xkv_recv.at[i, j - 1, h],
             device_id={"space": peer(j)},
@@ -119,8 +119,8 @@
         towards = 1 if side == RIGHT else -1
         owner = frame - towards * (step - 1)
         return pltpu.make_async_remote_copy(
-            src_ref=kv.at[owner, h, p, i] if src is None else src,
-            dst_ref=kv.at[owner, h, p, i],
+            src_ref=kv.at[owner, h, i, p] if src is None else src,
+            dst_ref=kv.at[owner, h, i, p],
             send_sem=z_send.at[side, step - 1, h, p, i],
             recv_sem=z_recv.at[side, step - 1, h, p, i],
             device_id={"frame": frame + towards},
@@ -141,8 +141,8 @@
         towards = 1 if side == RIGHT else -1
         owner = frame - towards * step
         return pltpu.make_async_remote_copy(
-            src_ref=kv.at[owner, h, p, i],
-            dst_ref=kv.at[owner, h, p, i],
+            src_ref=kv.at[owner, h, i, p],
+            dst_ref=kv.at[owner, h, i, p],
             send_sem=z_send.at[side, step - 1, h, p, i],
             recv_sem=z_recv.at[side, step - 1, h, p, i],
             device_id={"frame": frame - towards},
@@ -181,7 +181,11 @@
 
     each_head(open_queries)
 
-    dist[...] = jnp.abs(row_ref[...] - col_ref[...])
+    def row_of(axis):
+        at = lax.broadcasted_iota(jnp.int32, (tokens, tokens), axis).astype(jnp.float32)
+        return jnp.floor((at + 0.5) * (1.0 / columns))
+
+    dist[...] = jnp.abs(row_of(0) - row_of(1))
     top[...] = jnp.full(top.shape, NEG_FILL, jnp.float32)
     total[...] = jnp.zeros(total.shape, jnp.float32)
     acc[...] = jnp.zeros(acc.shape, jnp.float32)
@@ -200,85 +204,131 @@
 
     each_head(pass_parts)
 
+    def masked(h, g, at):
+        gap = jnp.abs(frame - g)
+        reach = jnp.where(flags_ref[frame, g] > 0, widths_ref[gap], -1).astype(jnp.float32)
+        cut = pl.ds(at, tile)
+        queries = qb[h].reshape(tokens, HEAD_DIM)[at : at + tile]
+        keys = kv[g, h, 0].reshape(tokens, HEAD_DIM)
+        scores = lax.dot_general(
+            queries, keys, (((1,), (1,)), ((), ())), preferred_element_type=jnp.float32
+        )
+        scores = jnp.where(dist[cut, :] <= reach, scores, NEG_FILL)
+        old_top = top[h, cut]
+        new_top = jnp.maximum(old_top, jnp.max(scores, axis=1, keepdims=True))
+        weights = jnp.exp2((scores - new_top) * SCALE)
+        keep = jnp.exp2((old_top - new_top) * SCALE)
+        top[h, cut] = new_top
+        total[h, cut] = total[h, cut] * keep + jnp.sum(weights, axis=1, keepdims=True)
+        return weights.astype(jnp.bfloat16), keep
+
+    def mixed(weights, h, g):
+        vals = kv[g, h, 1].reshape(tokens, HEAD_DIM)
+        return jnp.dot(weights, vals, preferred_element_type=jnp.float32)
+
     def update(h, g):
-        gap = jnp.abs(frame - g)
-        reach = jnp.where(flags_ref[frame, g] > 0, widths_ref[gap], -1)
-        keys = kv[g, h, :, 0].reshape(tokens, HEAD_DIM)
-        vals = kv[g, h, :, 1].reshape(tokens, HEAD_DIM)
-        queries = qb[h].reshape(tokens, HEAD_DIM)
         for at in range(0, tokens, tile):
             cut = pl.ds(at, tile)
-            scores = lax.dot_general(
-                queries[at : at + tile],
-                keys,
-                (((1,), (1,)), ((), ())),
-                preferred_element_type=jnp.float32,
-            )
-            scores = jnp.where(dist[cut, :] <= reach, scores, NEG_FILL)
-            old_top = top[h, cut]
-            new_top = jnp.maximum(old_top, jnp.max(scores, axis=1, keepdims=True))
-            weights = jnp.exp2((scores - new_top) * SCALE)
-            keep = jnp.exp2((old_top - new_top) * SCALE)
-            top[h, cut] = new_top
-            total[h, cut] = total[h, cut] * keep + jnp.sum(weights, axis=1, keepdims=True)
-            acc[h, cut] = acc[h, cut] * keep + jnp.dot(
-                weights.astype(jnp.bfloat16), vals, preferred_element_type=jnp.float32
-            )
-
-    def arrive(step, h):
+            weights, keep = masked(h, g, at)
+            acc[h, cut] = acc[h, cut] * keep + mixed(weights, h, g)
+
+    def await_block(side, step, h, i):
+        @pl.when(gets(side, step))
+        def _():
+            for p in range(parts):
+                landed(side, step, h, p, i).wait_recv()
+
+    def source(side, step):
+        return frame - step if side == RIGHT else frame + step
+
+    def near(step, h, relay):
+        for side in (LEFT, RIGHT):
+            for i in (0, 1):
+                await_block(side, step, h, i)
+            if relay:
+
+                @pl.when(gets(side, step) & can_send(side, step + 1))
+                def _():
+                    for i in (0, 1):
+                        for p in range(parts):
+                            hop(side, step + 1, h, p, i).start()
+
+    def blend(step, h):
         for side in (LEFT, RIGHT):
 
             @pl.when(gets(side, step))
             def _():
-                for p in range(parts):
-                    for i in (0, 1):
-                        landed(side, step, h, p, i).wait_recv()
-
-            if step < far:
-
-                @pl.when(gets(side, step) & can_send(side, step + 1))
+                update(h, source(side, step))
+
+    def first(h):
+        near(1, h, far > 1)
+        for copy in local_copies(h):
+            copy.wait()
+        for j in range(1, parts):
+            q_exchange(h, j).wait_recv()
+        update(h, frame)
+        blend(1, h)
+
+    each_head(first)
+
+    if far > 2:
+
+        @pl.loop(2, far)
+        def _(step):
+            def middle(h):
+                near(step, h, True)
+                blend(step, h)
+
+            each_head(middle)
+
+    def last(h):
+        for side in (LEFT, RIGHT):
+            if far > 1:
+                await_block(side, far, h, 0)
+
+                @pl.when(gets(side, far))
                 def _():
-                    for p in range(parts):
-                        for i in (0, 1):
-                            hop(side, step + 1, h, p, i).start()
-
-    def blend(step, h):
-        @pl.when(frame - step >= 0)
-        def _():
-            update(h, frame - step)
-
-        @pl.when(frame + step <= frames - 1)
-        def _():
-            update(h, frame + step)
-
-    for step in range(1, far + 1):
-
-        def advance(h, step=step):
-            arrive(step, h)
-            if step == 1:
-                for copy in local_copies(h):
-                    copy.wait()
-                for j in range(1, parts):
-                    q_exchange(h, j).wait_recv()
-                update(h, frame)
-            blend(step, h)
-            if step == far:
-                ob[h] = (acc[h] / total[h]).astype(jnp.bfloat16)
-                for j in range(1, parts):
-                    o_exchange(h, j).start()
-                o_keep(h).start()
-
-        each_head(advance)
+                    for at in range(0, tokens, tile):
+                        weights, keep = masked(h, source(side, far), at)
+                        wb[side, pl.ds(at, tile)] = weights
+                        acc[h, pl.ds(at, tile)] = acc[h, pl.ds(at, tile)] * keep
+
+        if far > 1:
+            for side in (LEFT, RIGHT):
+                await_block(side, far, h, 1)
+
+        def finish(p):
+            for at in range(0, rows, tile):
+                cut = pl.ds(pl.multiple_of(p * rows + at, tile), tile)
+                if far > 1:
+                    for side in (LEFT, RIGHT):
+
+                        @pl.when(gets(side, far))
+                        def _():
+                            acc[h, cut] = acc[h, cut] + mixed(
+                                wb[side, cut], h, source(side, far)
+                            )
+
+                ob[h, cut] = (acc[h, cut] / total[h, cut]).astype(jnp.bfloat16)
+
+        for j in range(1, parts):
+            finish(peer(j))
+            o_exchange(h, j).start()
+        finish(part)
+        o_keep(h).start()
+
+    each_head(last)
 
     def close_head(h):
-        mine = part * heads + h
         o_keep(h).wait()
         for j in range(1, parts):
             o_exchange(h, j).wait()
             q_exchange(h, j).wait_send()
             kv_exchange(h, j, 0, k_ref).wait_send()
             kv_exchange(h, j, 1, v_ref).wait_send()
-        for step in range(1, far + 1):
+
+        @pl.loop(1, far + 1)
+        def _(step):
             for side in (LEFT, RIGHT):
 
                 @pl.when(can_send(side, step))
@@ -297,23 +347,22 @@
     heads = features // HEAD_DIM // parts
     tokens = rows * parts
     far = frames - 2
-    token_rows = jnp.arange(tokens, dtype=jnp.int32) // columns
     flat = [a.reshape(rows, features) for a in (queries, keys, values)]
     any_spec = pl.BlockSpec(memory_space=pl.ANY)
-    vmem = pl.BlockSpec(memory_space=pltpu.VMEM)
     smem = pl.BlockSpec(memory_space=pltpu.SMEM)
     others = max(parts - 1, 1)
     dma = pltpu.SemaphoreType.DMA
     out = pl.pallas_call(
-        functools.partial(kernel, frames, parts, heads),
-        out_shape=jax.ShapeDtypeStruct((rows, features), jnp.bfloat16),
-        in_specs=[any_spec, any_spec, any_spec, smem, smem, vmem, vmem],
-        out_specs=any_spec,
+        functools.partial(kernel, frames, parts, heads, columns),
+        out_shape=pltpu.VMEM((rows, features), jnp.bfloat16),
+        in_specs=[any_spec, any_spec, any_spec, smem, smem],
+        out_specs=pl.BlockSpec(memory_space=pltpu.VMEM),
         scratch_shapes=[
-            pltpu.VMEM((frames, heads, parts, 2, rows, HEAD_DIM), jnp.bfloat16),
+            pltpu.VMEM((frames, heads, 2, parts, rows, HEAD_DIM), jnp.bfloat16),
             pltpu.VMEM((heads, parts, rows, HEAD_DIM), jnp.bfloat16),
             pltpu.VMEM((heads, tokens, HEAD_DIM), jnp.bfloat16),
-            pltpu.VMEM((tokens, tokens), jnp.int32),
+            pltpu.VMEM((tokens, tokens), jnp.float32),
+            pltpu.VMEM((2, tokens, tokens), jnp.bfloat16),
             pltpu.VMEM((heads, tokens, 1), jnp.float32),
             pltpu.VMEM((heads, tokens, 1), jnp.float32),
             pltpu.VMEM((heads, tokens, HEAD_DIM), jnp.float32),
@@ -329,7 +378,7 @@
             dma((others, heads)),
         ],
         compiler_params=pltpu.CompilerParams(collective_id=0, has_side_effects=True),
-    )(*flat, flags, widths, token_rows[:, None], token_rows[None, :])
+    )(*flat, flags, widths)
     return out.reshape(shape)
 
 

time: 67.5 us -> 63.8 us (0.945)
  other arithmetic: 1.31 us -> 0 us
  Pallas kernels: 64.1 us -> 62.8 us
  local copies, waits for them, and re-layouts: 1.92 us -> 0.82 us
    pallas_call x1, Pallas kernels: 64.1 us -> 62.8 us  [shards(): pl.pallas_call(functools.partial(kernel, frames, parts, heads, columns),...]
    select_n x2 -> x0, other arithmetic: 1.31 us -> none  [shards(): token_rows = jnp.arange(tokens, dtype=jnp.int32) // columns]
    unnamed x1, local copies, waits for them, and re-layouts: 1.92 us -> 0.82 us
where the time goes in v2:
time: 63.8 us; the launch traced here: 63.6 us
  Pallas kernels  62.8 us (98%)
  local copies, waits for them, and re-layouts  0.82 us (1%)
    pallas_call x1, Pallas kernels, shards(): pl.pallas_call(functools.partial(kernel, frames, parts, heads, columns),...  62.8 us

profile of v2, /device:TPU:0, one launch (start us, length us, event | category | flops | bytes accessed | tf_op | source)
XLA Modules:
  0.0 63.6 jit_solution(4565363569951654730)
XLA Ops:
  0.0 62.8 %shard_map.55 = bf16[192,1536]{1,0:T(8,128)(2,1)S(1)} custom-call(bf16[192,1536]{1,0:T(8,128)(2,1)} %bitcast.5, bf16[192,1536]{1,0:T(8,128)(2,1)} %bitcast.6, bf16[192,1536]{1,0:T(8,128)(2,1)} %bitcast.7, s32[4,4]{1,0:T(4,128)} %flags_ref.1, s32[4]{0:T(128)} %widths_ref.1), custom_call_target="tpu_custom_call" | custom-call | tf_op jit(solution)/shard_map/pallas_call | solution.py:355
  62.8 0.8 %copy.7 = bf16[1,4,48,1536]{3,2,1,0:T(8,128)(2,1)} copy(bf16[1,4,48,1536]{3,2,1,0:T(8,128)(2,1)S(1)} %bitcast.4) | data formatting | bytes 1179648

commit v3 on v2

--- a/solution.py
+++ b/solution.py
@@ -22,8 +22,8 @@
     q_ref,
     k_ref,
     v_ref,
-    flags_ref,
-    widths_ref,
+    flags_in,
+    widths_in,
     out_ref,
     kv,
     qb,
@@ -43,6 +43,9 @@
     o_local,
     o_send,
     o_recv,
+    flags_ref,
+    widths_ref,
+    table_sem,
 ):
     frame = lax.axis_index("frame")
     part = lax.axis_index("space")
@@ -173,6 +176,13 @@
 
     each_head(open_head)
 
+    tables = (
+        pltpu.make_async_copy(flags_in, flags_ref, table_sem.at[0]),
+        pltpu.make_async_copy(widths_in, widths_ref, table_sem.at[1]),
+    )
+    for copy in tables:
+        copy.start()
+
     def open_queries(h):
         for copy in local_copies(h):
             copy.start()
@@ -203,6 +213,8 @@
                         hop(side, 1, h, p, i).start()
 
     each_head(pass_parts)
+    for copy in tables:
+        copy.wait()
 
     def masked(h, g, at):
         gap = jnp.abs(frame - g)
@@ -349,13 +361,12 @@
     far = frames - 2
     flat = [a.reshape(rows, features) for a in (queries, keys, values)]
     any_spec = pl.BlockSpec(memory_space=pl.ANY)
-    smem = pl.BlockSpec(memory_space=pltpu.SMEM)
     others = max(parts - 1, 1)
     dma = pltpu.SemaphoreType.DMA
     out = pl.pallas_call(
         functools.partial(kernel, frames, parts, heads, columns),
         out_shape=pltpu.VMEM((rows, features), jnp.bfloat16),
-        in_specs=[any_spec, any_spec, any_spec, smem, smem],
+        in_specs=[any_spec] * 5,
         out_specs=pl.BlockSpec(memory_space=pltpu.VMEM),
         scratch_shapes=[
             pltpu.VMEM((frames, heads, 2, parts, rows, HEAD_DIM), jnp.bfloat16),
@@ -376,6 +387,9 @@
             dma((heads,)),
             dma((others, heads)),
             dma((others, heads)),
+            pltpu.SMEM(flags.shape, jnp.int32),
+            pltpu.SMEM(widths.shape, jnp.int32),
+            dma((2,)),
         ],
         compiler_params=pltpu.CompilerParams(collective_id=0, has_side_effects=True),
     )(*flat, flags, widths)

time: 63.8 us -> 63 us (0.987)
  Pallas kernels: 62.8 us -> 62 us
    pallas_call x1, Pallas kernels: 62.8 us -> 62 us  [shards(): pl.pallas_call(functools.partial(kernel, frames, parts, heads, columns),...]
where the time goes in v3:
time: 63 us; the launch traced here: 62.9 us
  Pallas kernels  62 us (98%)
  local copies, waits for them, and re-layouts  0.82 us (1%)
    pallas_call x1, Pallas kernels, shards(): pl.pallas_call(functools.partial(kernel, frames, parts, heads, columns),...  62 us

profile of v3, /device:TPU:0, one launch (start us, length us, event | category | flops | bytes accessed | tf_op | source)
XLA Modules:
  0.0 62.9 jit_solution(11431248678801232551)
XLA Ops:
  0.0 62.0 %shard_map.55 = bf16[192,1536]{1,0:T(8,128)(2,1)S(1)} custom-call(bf16[192,1536]{1,0:T(8,128)(2,1)} %bitcast.5, bf16[192,1536]{1,0:T(8,128)(2,1)} %bitcast.6, bf16[192,1536]{1,0:T(8,128)(2,1)} %bitcast.7, s32[4,4]{1,0:T(4,128)} %flags_in.1, s32[4]{0:T(128)} %widths_in.1), custom_call_target="tpu_custom_call" | custom-call | tf_op jit(solution)/shard_map/pallas_call | solution.py:366
  62.0 0.8 %copy.7 = bf16[1,4,48,1536]{3,2,1,0:T(8,128)(2,1)} copy(bf16[1,4,48,1536]{3,2,1,0:T(8,128)(2,1)S(1)} %bitcast.4) | data formatting | bytes 1179648

commit v4 on v3

--- a/solution.py
+++ b/solution.py
@@ -305,6 +305,7 @@
                         wb[side, pl.ds(at, tile)] = weights
                         acc[h, pl.ds(at, tile)] = acc[h, pl.ds(at, tile)] * keep
 
+        total[h] = 1.0 / total[h]
         if far > 1:
             for side in (LEFT, RIGHT):
                 await_block(side, far, h, 1)
@@ -321,7 +322,7 @@
                                 wb[side, cut], h, source(side, far)
                             )
 
-                ob[h, cut] = (acc[h, cut] / total[h, cut]).astype(jnp.bfloat16)
+                ob[h, cut] = (acc[h, cut] * total[h, cut]).astype(jnp.bfloat16)
 
         for j in range(1, parts):
             finish(peer(j))

time: 63 us -> 63 us (level)
  no operation moved by 1% of the time
where the time goes in v4:
time: 63 us; the launch traced here: 62.9 us
  Pallas kernels  62 us (98%)
  local copies, waits for them, and re-layouts  0.82 us (1%)
    pallas_call x1, Pallas kernels, shards(): pl.pallas_call(functools.partial(kernel, frames, parts, heads, columns),...  62 us

profile of v4, /device:TPU:0, one launch (start us, length us, event | category | flops | bytes accessed | tf_op | source)
XLA Modules:
  0.0 62.9 jit_solution(9147277733952223685)
XLA Ops:
  0.0 62.0 %shard_map.55 = bf16[192,1536]{1,0:T(8,128)(2,1)S(1)} custom-call(bf16[192,1536]{1,0:T(8,128)(2,1)} %bitcast.5, bf16[192,1536]{1,0:T(8,128)(2,1)} %bitcast.6, bf16[192,1536]{1,0:T(8,128)(2,1)} %bitcast.7, s32[4,4]{1,0:T(4,128)} %flags_in.1, s32[4]{0:T(128)} %widths_in.1), custom_call_target="tpu_custom_call" | custom-call | tf_op jit(solution)/shard_map/pallas_call | solution.py:367
  62.0 0.8 %copy.7 = bf16[1,4,48,1536]{3,2,1,0:T(8,128)(2,1)} copy(bf16[1,4,48,1536]{3,2,1,0:T(8,128)(2,1)S(1)} %bitcast.4) | data formatting | bytes 1179648
